TPU v7x, 512 devices: a whole 4x4x16 slice. The times are simulated.
512 devices in a mesh: dp: 8 (over z_hi, y), ctx: 64 (over z_lo, x, core).
Axes of the slice: x: 4, y: 4, z: 16 (z_hi: 2, z_lo: 8; z = z_hi * 8 + z_lo), core: 2. Of those that a mesh axis runs over, the one named last changes fastest.
Arguments:
- queries: bfloat16 [8, 8192, 1024], P('dp', 'ctx'), may hold values from -6 to 6
- keys: bfloat16 [8, 8192, 1024], P('dp', 'ctx'), may hold values from -6 to 6
- values: bfloat16 [8, 8192, 1024], P('dp', 'ctx'), may hold values from -6 to 6
- rel_bias: float32 [16, 769], replicated, may hold values from -8 to 8
- grad_out: bfloat16 [8, 8192, 1024], P('dp', 'ctx'), may hold values from -6 to 6
Outputs:
- attended: bfloat16 [8, 8192, 1024], P('dp', 'ctx')
- grad_queries: bfloat16 [8, 8192, 1024], P('dp', 'ctx')
- grad_keys: bfloat16 [8, 8192, 1024], P('dp', 'ctx')
- grad_values: bfloat16 [8, 8192, 1024], P('dp', 'ctx')
- grad_bias: float32 [16, 769], replicated
All inputs are finite; a program needn't handle non-finite values.
Results may differ from a plain program's by a relative error of at most 0.024.
Values may be sent and summed in bfloat16 or wider, within the bound.
No kernel may reach another device: no remote copies, remote signals or barrier semaphores. Data moves between devices by JAX's collectives and lax.ppermute only.
A program may use at most 128 MiB of HBM per device.

v0:
```python
import math

import jax
import jax.numpy as jnp
from jax import lax
from jax.experimental import pallas as pl
from jax.experimental.pallas import tpu as pltpu
from jax.sharding import Mesh, PartitionSpec as P

HEADS = 16
HEAD = 64
FR = 128
NB = 3
CONTEXT = NB * FR
MEMB = 8
FAR = 2
CORES = 2
ROWS = MEMB * FR
PAD_ROWS = ROWS + 2 * CONTEXT
TILE = 256
WIN = TILE + 2 * CONTEXT
CH = 128
NCH = WIN // CH
DIAGS = 2 * NB + 1
LANES = 128
EXCLUDED = -1e30
SCALE = 1.0 / math.sqrt(HEAD)
F32 = jnp.float32
BF16 = jnp.bfloat16

NN = (((1,), (0,)), ((), ()))
NT = (((1,), (1,)), ((), ()))


def dot(a, b, dims):
    return lax.dot_general(a, b, dims, preferred_element_type=F32)


def attention_kernel(
    place, kv_left, kv_mid, kv_right, qd, bias_row,
    od, dkv, dkv_left, dkv_right, bias_grad,
    kv, kv_t, qd_t, table, scores, probs, dscores, key_acc, value_acc, diag_acc,
    od_t, sems,
):
    copies = [
        pltpu.make_async_copy(kv_left, kv.at[pl.ds(0, CONTEXT)], sems.at[0]),
        pltpu.make_async_copy(kv_mid, kv.at[pl.ds(CONTEXT, ROWS)], sems.at[1]),
        pltpu.make_async_copy(kv_right, kv.at[pl.ds(CONTEXT + ROWS, CONTEXT)], sems.at[2]),
    ]
    for copy in copies:
        copy.start()
    first = place[0] == 0
    last = place[0] == place[1] - 1
    key_acc[...] = jnp.zeros_like(key_acc)
    value_acc[...] = jnp.zeros_like(value_acc)
    diag_acc[...] = jnp.zeros_like(diag_acc)
    for h in range(2):
        for c in range(NCH):
            start = (-LANES * (c + 1)) % (5 * TILE)
            parts = [
                bias_row[h : h + 1, (start + LANES * n) % (5 * TILE) : (start + LANES * n) % (5 * TILE) + LANES]
                for n in range(3)
            ]
            wide = jnp.broadcast_to(jnp.concatenate(parts, axis=1), (CH, 3 * LANES))
            turned = pltpu.roll(wide, 0, 1, stride=1, stride_axis=0)
            table[h, pl.ds(c * CH, CH), :] = turned[:, LANES:]
    qd_t[...] = qd[...].T
    for copy in copies:
        copy.wait()
    kv_t[...] = kv[...].T

    lane = lax.broadcasted_iota(jnp.int32, (TILE, LANES), 1)
    small = jnp.asarray(SCALE, BF16)

    def rows(c):
        return pl.ds(c * CH, CH)

    class Part:
        def __init__(self, base, h, n):
            self.base, self.h, self.n, self.m = base, h, n % 3, n % 2
            self.o = (base // TILE) % 2
            self.head = pl.ds(h * HEAD, HEAD)
            self.own = (lane >= h * HEAD) & (lane < (h + 1) * HEAD)

        def score_start(self):
            q = qd[pl.ds(self.base, TILE), :LANES] * small
            self.q = jnp.where(self.own, q, jnp.zeros_like(q))
            self.top8 = jnp.full((8, TILE), EXCLUDED, F32)

        def score(self, c):
            at = self.base + c * CH
            s = dot(kv[pl.ds(at, CH), :LANES], self.q, NT) + table[self.h, rows(c), :]
            if c < NB or c >= NCH - NB:
                bad = (first & (at < CONTEXT)) | (last & (at >= CONTEXT + ROWS))
                s = jnp.where(bad, EXCLUDED, s)
            scores[self.n, rows(c), :] = s
            self.top8 = jnp.maximum(self.top8, jnp.max(s.reshape(CH // 8, 8, TILE), axis=0))

        def prob_start(self):
            self.top = jnp.max(self.top8, axis=0, keepdims=True)
            self.sum8 = jnp.zeros((8, TILE), F32)

        def prob(self, c):
            p = jnp.exp(scores[self.n, rows(c), :] - self.top)
            scores[self.n, rows(c), :] = p
            probs[self.n, rows(c), :] = p.astype(BF16)
            self.sum8 = self.sum8 + jnp.sum(p.reshape(CH // 8, 8, TILE), axis=0)

        def output(self):
            self.inv = 1.0 / jnp.sum(self.sum8, axis=0, keepdims=True)
            v_t = kv_t[pl.ds(LANES + self.h * HEAD, HEAD), pl.ds(self.base, WIN)]
            out_t = (dot(v_t, probs[self.n], NN) * self.inv).astype(BF16)
            od_t[self.o, self.head, :] = out_t
            d_t = qd_t[pl.ds(LANES + self.h * HEAD, HEAD), pl.ds(self.base, TILE)].astype(F32)
            self.delta = jnp.sum(out_t.astype(F32) * d_t, axis=0, keepdims=True) * self.inv
            self.d_scaled = (d_t * self.inv).astype(BF16)
            d = qd[pl.ds(self.base, TILE), LANES:]
            self.d = jnp.where(self.own, d, jnp.zeros_like(d))

        def dscore(self, c):
            at = self.base + c * CH
            dp = dot(kv[pl.ds(at, CH), LANES:], self.d, NT)
            ds = scores[self.n, rows(c), :] * (dp * self.inv - self.delta)
            dscores[self.m, rows(c), :] = ds.astype(BF16)
            for i in range(TILE // CH):
                k = i - c + DIAGS - 1
                if 0 <= k < DIAGS:
                    cols = slice((k + 1) * LANES, (k + 2) * LANES)
                    diag_acc[self.h, :, cols] += ds[:, i * CH : (i + 1) * CH]

        def value_grad(self, c):
            at, two = pl.ds(self.base + c * TILE, TILE), pl.ds(c * TILE, TILE)
            value_acc[self.head, at] += dot(self.d_scaled, probs[self.n, two, :], NT)

        def key_grad(self, c):
            at, two = pl.ds(self.base + c * TILE, TILE), pl.ds(c * TILE, TILE)
            q_t = qd_t[self.head, pl.ds(self.base, TILE)] * small
            key_acc[self.head, at] += dot(q_t, dscores[self.m, two, :], NT)

        def query_grad(self):
            k_t = kv_t[self.head, pl.ds(self.base, WIN)]
            dq_t = (dot(k_t, dscores[self.m], NN) * SCALE).astype(BF16)
            od_t[self.o, pl.ds(LANES + self.h * HEAD, HEAD), :] = dq_t

    parts = [Part(t * TILE, h, t * 2 + h) for t in range(ROWS // TILE) for h in range(2)]
    for step in range(len(parts) + 3):
        now = [parts[step - lag] if 0 <= step - lag < len(parts) else None for lag in range(4)]
        if now[0]:
            now[0].score_start()
        if now[1]:
            now[1].prob_start()
        if now[2]:
            now[2].output()
        for c in range(NCH):
            if now[0]:
                now[0].score(c)
            if now[1]:
                now[1].prob(c)
            if now[2]:
                now[2].dscore(c)
            if now[3] and c % 2:
                now[3].value_grad(c // 2)
                now[3].key_grad(c // 2)
        if now[3]:
            now[3].query_grad()
            if now[3].h == 1:
                od[pl.ds(now[3].base, TILE), :] = od_t[(now[3].base // TILE) % 2].T

    for n, acc in enumerate((key_acc, value_acc)):
        cols = slice(n * LANES, (n + 1) * LANES)
        dkv_left[:, cols] = acc[:, :CONTEXT].astype(BF16).T
        dkv[:, cols] = acc[:, CONTEXT : CONTEXT + ROWS].astype(BF16).T
        dkv_right[:, cols] = acc[:, CONTEXT + ROWS :].astype(BF16).T

    wide = (DIAGS + 1) * LANES
    part = diag_acc[...]
    size = CH
    while size > 8:
        size //= 2
        part = part[:, :size] + pltpu.roll(part[:, size:], wide - size, 2)
    sub = lax.broadcasted_iota(jnp.int32, (2, 8, wide), 1)
    for step in (4, 2, 1):
        part = jnp.where((sub & step) != 0, pltpu.roll(part, wide - step, 2), part)
    total = jnp.sum(part, axis=1)
    bias_grad[...] = total[:, LANES:]


def attention(place, kv_left, kv_mid, kv_right, qd, bias_row):
    vmem = pl.BlockSpec(memory_space=pltpu.VMEM)
    hbm = pl.BlockSpec(memory_space=pl.ANY)
    return pl.pallas_call(
        attention_kernel,
        out_shape=(
            jax.ShapeDtypeStruct((ROWS, 2 * LANES), BF16),
            jax.ShapeDtypeStruct((ROWS, 2 * LANES), BF16),
            jax.ShapeDtypeStruct((CONTEXT, 2 * LANES), BF16),
            jax.ShapeDtypeStruct((CONTEXT, 2 * LANES), BF16),
            jax.ShapeDtypeStruct((2, DIAGS * LANES), F32),
        ),
        in_specs=[pl.BlockSpec(memory_space=pltpu.SMEM), hbm, hbm, hbm, vmem, vmem],
        out_specs=(vmem,) * 5,
        scratch_shapes=[
            pltpu.VMEM((PAD_ROWS, 2 * LANES), BF16),
            pltpu.VMEM((2 * LANES, PAD_ROWS), BF16),
            pltpu.VMEM((2 * LANES, ROWS), BF16),
            pltpu.VMEM((2, WIN, TILE), F32),
            pltpu.VMEM((3, WIN, TILE), F32),
            pltpu.VMEM((3, WIN, TILE), BF16),
            pltpu.VMEM((2, WIN, TILE), BF16),
            pltpu.VMEM((LANES, PAD_ROWS), F32),
            pltpu.VMEM((LANES, PAD_ROWS), F32),
            pltpu.VMEM((2, CH, (DIAGS + 1) * LANES), F32),
            pltpu.VMEM((2, 2 * LANES, TILE), BF16),
            pltpu.SemaphoreType.DMA((3,)),
        ],
        compiler_params=pltpu.CompilerParams(vmem_limit_bytes=40 * 2**20),
        cost_estimate=pl.CostEstimate(flops=3 * 10**9, bytes_accessed=6 * 2**20, transcendentals=2 * 10**6),
        name="attention",
    )(place, kv_left, kv_mid, kv_right, qd, bias_row)


def pack_kernel(a, b, out):
    for m in range(MEMB):
        cols = slice(m * LANES, (m + 1) * LANES)
        out[m, :, :LANES] = a[0, :, cols]
        out[m, :, LANES:] = b[0, :, cols]


def pack(a, b):
    vmem = pl.BlockSpec(memory_space=pltpu.VMEM)
    return pl.pallas_call(
        pack_kernel,
        out_shape=jax.ShapeDtypeStruct((MEMB, FR, 2 * LANES), BF16),
        in_specs=[vmem, vmem],
        out_specs=vmem,
        cost_estimate=pl.CostEstimate(flops=0, bytes_accessed=2**20, transcendentals=0),
        name="pack",
    )(a, b)


def unpack_kernel(merged, *outs):
    for m in range(MEMB):
        for n, out in enumerate(outs):
            out[0, :, m * LANES : (m + 1) * LANES] = merged[m, :, n * LANES : (n + 1) * LANES]


def unpack(merged):
    vmem = pl.BlockSpec(memory_space=pltpu.VMEM)
    return pl.pallas_call(
        unpack_kernel,
        out_shape=(jax.ShapeDtypeStruct((1, FR, MEMB * LANES), BF16),) * 4,
        in_specs=[vmem],
        out_specs=(vmem,) * 4,
        cost_estimate=pl.CostEstimate(flops=0, bytes_accessed=2 * 2**20, transcendentals=0),
        name="unpack",
    )(merged)


def join_kernel(od, dkv, from_left, from_right, out):
    def add(a, b):
        return (a.astype(F32) + b.astype(F32)).astype(BF16)

    for m in range(MEMB):
        mine = pl.ds(m * FR, FR)
        out[m, :, : 2 * LANES] = od[mine]
        if m < NB:
            out[m, :, 2 * LANES :] = add(dkv[mine], from_left[mine])
        elif m >= MEMB - NB:
            out[m, :, 2 * LANES :] = add(dkv[mine], from_right[pl.ds((m - MEMB + NB) * FR, FR)])
        else:
            out[m, :, 2 * LANES :] = dkv[mine]


def join(od, dkv, from_left, from_right):
    vmem = pl.BlockSpec(memory_space=pltpu.VMEM)
    return pl.pallas_call(
        join_kernel,
        out_shape=jax.ShapeDtypeStruct((MEMB, FR, 4 * LANES), BF16),
        in_specs=[vmem] * 4,
        out_specs=vmem,
        cost_estimate=pl.CostEstimate(flops=2**18, bytes_accessed=2 * 2**20, transcendentals=0),
        name="join",
    )(od, dkv, from_left, from_right)


def to_all(x, axes):
    return lax.all_to_all(x, axes, 0, 0, tiled=True)


def shifted(x, by):
    n = lax.axis_size("grp")
    return lax.ppermute(x, "grp", [(i, i + by) for i in range(n) if 0 <= i + by < n])


def body(queries, keys, values, rel_bias, grad_out):
    groups = lax.axis_size("grp")
    kv = to_all(pack(keys, values), ("x", "core"))
    left = shifted(kv[MEMB - NB :], 1)
    right = shifted(kv[:NB], -1)
    qd = to_all(pack(queries, grad_out), ("x", "core"))
    member = lax.axis_index(("x", "core"))
    mine = lax.dynamic_slice_in_dim(rel_bias, 2 * member, 2, axis=0)
    gap = jnp.full((2, 2 * TILE - 1), EXCLUDED, F32)
    bias_row = jnp.concatenate([mine[:, 2 * CONTEXT :], gap, mine[:, : 2 * CONTEXT]], axis=1)
    place = jnp.stack([lax.axis_index("grp"), jnp.int32(groups)])
    od, dkv, dleft, dright, dbias = attention(
        place,
        left.reshape(CONTEXT, 2 * LANES),
        kv.reshape(ROWS, 2 * LANES),
        right.reshape(CONTEXT, 2 * LANES),
        qd.reshape(ROWS, 2 * LANES),
        bias_row,
    )
    from_right = shifted(dleft, -1)
    from_left = shifted(dright, 1)
    column = lax.axis_size(("far", "grp"))
    column = to_all(jnp.broadcast_to(dbias[None], (column,) + dbias.shape), ("far", "grp"))
    grads = join(od, dkv, from_left, from_right)
    grads, column = lax.optimization_barrier((grads, column))
    merged = to_all(grads, ("x", "core"))
    one = lax.psum(jnp.sum(column, axis=0), "row")
    one, merged = lax.optimization_barrier((one, merged))
    every = to_all(jnp.broadcast_to(one[None], (MEMB,) + one.shape), ("x", "core"))
    attended, grad_queries, grad_keys, grad_values = unpack(merged)
    grad_bias = every.reshape(HEADS, DIAGS * LANES)[:, : 2 * CONTEXT + 1]
    return (attended, grad_queries, grad_keys, grad_values, grad_bias)


def solution(mesh):
    dp, ctx = mesh.devices.shape
    split = (FAR, dp // FAR, ctx // MEMB, MEMB // CORES, CORES)
    fine = Mesh(mesh.devices.reshape(split), ("far", "row", "grp", "x", "core"))
    placed = P(("far", "row"), ("grp", "x", "core"), None)
    return jax.shard_map(
        body,
        mesh=fine,
        in_specs=(placed, placed, placed, P(), placed),
        out_specs=(placed, placed, placed, placed, P()),
        check_vma=False,
    )
```

profile of v0, /device:TPU:1, one launch (start us, length us, event | category | flops | bytes accessed | tf_op | source)
XLA Modules:
  0.0 105.9 jit_solution(17107129320863647092)
XLA Ops:
  0.6 1.9 %pack.2 = bf16[8,128,256]{2,1,0:T(8,128)(2,1)} custom-call(bf16[1,128,1024]{2,1,0:T(8,128)(2,1)} %a.2, bf16[1,128,1024]{2,1,0:T(8,128)(2,1)} %b.2), custom_call_target="tpu_custom_call" | custom-call | bytes 1048576 | tf_op jit(solution)/shard_map/pack/pallas_call | solution.py:231
  2.5 10.3 %all-to-all-start = ((bf16[8,128,256]{2,1,0:T(8,128)(2,1)}), bf16[8,128,256]{2,1,0:T(8,128)(2,1)S(1)}, u32[]{:S(2)}, u32[]{:S(2)}) async-start(bf16[8,128,256]{2,1,0:T(8,128)(2,1)} %pack.2), calls=%async_computation | async-start | bytes 1048576 | tf_op jit(solution)/shard_map/all_to_all | solution.py:287
  12.8 1.9 %pack.3 = bf16[8,128,256]{2,1,0:T(8,128)(2,1)} custom-call(bf16[1,128,1024]{2,1,0:T(8,128)(2,1)} %a.3, bf16[1,128,1024]{2,1,0:T(8,128)(2,1)} %b.3), custom_call_target="tpu_custom_call" | custom-call | bytes 1048576 | tf_op jit(solution)/shard_map/pack/pallas_call | solution.py:231
  14.7 0.8 dynamic-slice
  15.5 6.8 %all-to-all-done = bf16[8,128,256]{2,1,0:T(8,128)(2,1)S(1)} async-done(((bf16[8,128,256]{2,1,0:T(8,128)(2,1)}), bf16[8,128,256]{2,1,0:T(8,128)(2,1)S(1)}, u32[]{:S(2)}, u32[]{:S(2)}) %all-to-all-start) | async-done | bytes 524320 | tf_op jit(solution)/shard_map/all_to_all | solution.py:287
  22.3 4.3 %all-to-all-start.1 = ((bf16[8,128,256]{2,1,0:T(8,128)(2,1)}), bf16[8,128,256]{2,1,0:T(8,128)(2,1)S(1)}, u32[]{:S(2)}, u32[]{:S(2)}) async-start(bf16[8,128,256]{2,1,0:T(8,128)(2,1)} %pack.3), calls=%async_computation.1 | async-start | bytes 1048576 | tf_op jit(solution)/shard_map/all_to_all | solution.py:287
  26.6 1.3 %collective-permute-start.1 = (bf16[3,128,256]{2,1,0:T(8,128)(2,1)S(1)}, bf16[3,128,256]{2,1,0:T(8,128)(2,1)S(1)}, u32[]{:S(2)}, u32[]{:S(2)}) collective-permute-start(bf16[3,128,256]{2,1,0:T(8,128)(2,1)S(1)} %get-tuple-element.31), channel_id=1, source_target_pairs={{8,0},{16,8},{24,16},{32,24},{40,32},{48,40},{56,48},{9,1},{17,9},... | collective-permute-start | bytes 589832 | tf_op jit(solution)/shard_map/ppermute | solution.py:292
  27.9 4.0 %collective-permute-start = (bf16[3,128,256]{2,1,0:T(8,128)(2,1)S(1)}, bf16[3,128,256]{2,1,0:T(8,128)(2,1)S(1)}, u32[]{:S(2)}, u32[]{:S(2)}) collective-permute-start(bf16[3,128,256]{2,1,0:T(8,128)(2,1)S(1)} %get-tuple-element.32), channel_id=1, source_target_pairs={{0,8},{8,16},{16,24},{24,32},{32,40},{40,48},{48,56},{1,9},{9,17},... | collective-permute-start | bytes 589832 | tf_op jit(solution)/shard_map/ppermute | solution.py:292
  32.0 0.8 constant_dynamic-slice_fusion
  32.7 0.1 concatenate.3.bias_row
  32.8 0.1 pad_add_fusion.place
  32.9 3.2 %all-to-all-done.1 = bf16[8,128,256]{2,1,0:T(8,128)(2,1)S(1)} async-done(((bf16[8,128,256]{2,1,0:T(8,128)(2,1)}), bf16[8,128,256]{2,1,0:T(8,128)(2,1)S(1)}, u32[]{:S(2)}, u32[]{:S(2)}) %all-to-all-start.1) | async-done | bytes 524320 | tf_op jit(solution)/shard_map/all_to_all | solution.py:287
  36.1 0.0 collective-permute-done.1
  36.1 0.0 collective-permute-done
  36.1 9.7 %attention.1 = (bf16[1024,256]{1,0:T(8,128)(2,1)S(1)}, bf16[1024,256]{1,0:T(8,128)(2,1)S(1)}, bf16[384,256]{1,0:T(8,128)(2,1)S(1)}, bf16[384,256]{1,0:T(8,128)(2,1)S(1)}, f32[2,896]{1,0:T(2,128)S(1)}) custom-call(s32[2]{0:T(128)S(1)} %pad_add_fusion.place, bf16[384,256]{1,0:T(8,128)(2,1)S(1)} %bitcast.9, bf16[1024,256]{1,0:T(8,128)(2,1)S(1)} %bitcast.6, ...), custom_call_target="tpu_custom_call" | custom-call | flops 3000000000 | bytes 6291456 | tf_op jit(solution)/shard_map/attention/pallas_call | solution.py:191
  45.8 0.0 copy-start
  45.8 0.8 copy-done
  46.7 0.0 copy-start.1
  46.7 0.8 copy-done.1
  47.5 0.7 broadcast_in_dim.7
  48.2 11.2 %all-to-all-start.2 = ((f32[16,2,896]{2,1,0:T(2,128)}), f32[16,2,896]{2,1,0:T(2,128)S(1)}, u32[]{:S(2)}, u32[]{:S(2)}) async-start(f32[16,2,896]{2,1,0:T(2,128)} %broadcast_in_dim.7), calls=%async_computation.2 | async-start | bytes 229376 | tf_op jit(solution)/shard_map/all_to_all | solution.py:287
  59.4 3.3 %collective-permute-start.2 = (bf16[384,256]{1,0:T(8,128)(2,1)S(1)}, bf16[384,256]{1,0:T(8,128)(2,1)S(1)}, u32[]{:S(2)}, u32[]{:S(2)}) collective-permute-start(bf16[384,256]{1,0:T(8,128)(2,1)S(1)} %get-tuple-element.20), channel_id=1, source_target_pairs={{0,8},{8,16},{16,24},{24,32},{32,40},{40,48},{48,56},{1,9},{9,17},... | collective-permute-start | bytes 589832 | tf_op jit(solution)/shard_map/ppermute | solution.py:292
  62.6 1.3 %collective-permute-start.3 = (bf16[384,256]{1,0:T(8,128)(2,1)S(1)}, bf16[384,256]{1,0:T(8,128)(2,1)S(1)}, u32[]{:S(2)}, u32[]{:S(2)}) collective-permute-start(bf16[384,256]{1,0:T(8,128)(2,1)S(1)} %get-tuple-element.21), channel_id=1, source_target_pairs={{8,0},{16,8},{24,16},{32,24},{40,32},{48,40},{56,48},{9,1},{17,9},... | collective-permute-start | bytes 589832 | tf_op jit(solution)/shard_map/ppermute | solution.py:292
  63.9 5.3 %collective-permute-done.2.from_left = bf16[384,256]{1,0:T(8,128)(2,1)S(1)} collective-permute-done((bf16[384,256]{1,0:T(8,128)(2,1)S(1)}, bf16[384,256]{1,0:T(8,128)(2,1)S(1)}, u32[]{:S(2)}, u32[]{:S(2)}) %collective-permute-start.2) | collective-permute-done | bytes 196640 | tf_op jit(solution)/shard_map/ppermute | solution.py:292
  69.2 0.0 copy-start.3
  69.2 2.1 %collective-permute-done.3.from_right = bf16[384,256]{1,0:T(8,128)(2,1)S(1)} collective-permute-done((bf16[384,256]{1,0:T(8,128)(2,1)S(1)}, bf16[384,256]{1,0:T(8,128)(2,1)S(1)}, u32[]{:S(2)}, u32[]{:S(2)}) %collective-permute-start.3) | collective-permute-done | bytes 196640 | tf_op jit(solution)/shard_map/ppermute | solution.py:292
  71.3 0.0 copy-start.4
  71.3 0.0 copy-done.3
  71.3 0.7 copy-done.4
  72.0 2.4 %join.1 = bf16[8,128,512]{2,1,0:T(8,128)(2,1)} custom-call(bf16[1024,256]{1,0:T(8,128)(2,1)} %copy-done, bf16[1024,256]{1,0:T(8,128)(2,1)} %copy-done.1, bf16[384,256]{1,0:T(8,128)(2,1)} %copy-done.3, bf16[384,256]{1,0:T(8,128)(2,1)} %copy-done.4), custom_call_target="tpu_custom_call" | custom-call | flops 262144 | bytes 2097152 | tf_op jit(solution)/shard_map/join/pallas_call | solution.py:276
  74.3 0.0 all-to-all-done.2
  74.3 6.1 %all-to-all-start.3 = ((bf16[8,128,512]{2,1,0:T(8,128)(2,1)}), bf16[8,128,512]{2,1,0:T(8,128)(2,1)S(1)}, u32[]{:S(2)}, u32[]{:S(2)}) async-start(bf16[8,128,512]{2,1,0:T(8,128)(2,1)} %join.1), calls=%async_computation.3 | async-start | bytes 2097152 | tf_op jit(solution)/shard_map/all_to_all | solution.py:287
  80.5 0.1 reduce_sum.9
  80.5 9.4 %psum.7 = f32[2,896]{1,0:T(2,128)S(1)} all-reduce(f32[2,896]{1,0:T(2,128)S(1)} %reduce_sum.9), channel_id=1, replica_groups=mesh['far'=2,'row'=4,'grp'=8,'x'=4,'core'=2] {'row'}, use_global_device_ids=true, to_apply=%region_1.0 | all-reduce | flops 1792 | bytes 14336 | tf_op jit(solution)/shard_map/psum | solution.py:321
  89.9 5.6 %all-to-all-done.3.merged = bf16[8,128,512]{2,1,0:T(8,128)(2,1)S(1)} async-done(((bf16[8,128,512]{2,1,0:T(8,128)(2,1)}), bf16[8,128,512]{2,1,0:T(8,128)(2,1)S(1)}, u32[]{:S(2)}, u32[]{:S(2)}) %all-to-all-start.3) | async-done | bytes 1048608 | tf_op jit(solution)/shard_map/all_to_all | solution.py:287
  95.6 0.0 copy-start.2
  95.6 0.7 broadcast_in_dim.8
  96.3 4.1 %all-to-all-start.4 = ((f32[8,2,896]{2,1,0:T(2,128)}), f32[8,2,896]{2,1,0:T(2,128)S(1)}, u32[]{:S(2)}, u32[]{:S(2)}) async-start(f32[8,2,896]{2,1,0:T(2,128)} %broadcast_in_dim.8), calls=%async_computation.4 | async-start | bytes 114688 | tf_op jit(solution)/shard_map/all_to_all | solution.py:287
  100.4 0.0 copy-done.2
  100.4 2.5 %unpack.1 = (bf16[1,128,1024]{2,1,0:T(8,128)(2,1)}, bf16[1,128,1024]{2,1,0:T(8,128)(2,1)}, bf16[1,128,1024]{2,1,0:T(8,128)(2,1)}, bf16[1,128,1024]{2,1,0:T(8,128)(2,1)}) custom-call(bf16[8,128,512]{2,1,0:T(8,128)(2,1)} %copy-done.2), custom_call_target="tpu_custom_call" | custom-call | bytes 2097152 | tf_op jit(solution)/shard_map/unpack/pallas_call | solution.py:249
  102.9 2.4 %all-to-all-done.4 = f32[8,2,896]{2,1,0:T(2,128)S(1)} async-done(((f32[8,2,896]{2,1,0:T(2,128)}), f32[8,2,896]{2,1,0:T(2,128)S(1)}, u32[]{:S(2)}, u32[]{:S(2)}) %all-to-all-start.4) | async-done | bytes 57376 | tf_op jit(solution)/shard_map/all_to_all | solution.py:287
  105.2 0.7 reshape.31
  (2 shorter events, 0.0 us)
Async XLA Ops:
  2.5 19.8 %all-to-all-start = ((bf16[8,128,256]{2,1,0:T(8,128)(2,1)}), bf16[8,128,256]{2,1,0:T(8,128)(2,1)S(1)}, u32[]{:S(2)}, u32[]{:S(2)}) async-start(bf16[8,128,256]{2,1,0:T(8,128)(2,1)} %pack.2), calls=%async_computation | async-start | bytes 1048576 | tf_op jit(solution)/shard_map/all_to_all | solution.py:287
  22.3 13.8 %all-to-all-start.1 = ((bf16[8,128,256]{2,1,0:T(8,128)(2,1)}), bf16[8,128,256]{2,1,0:T(8,128)(2,1)S(1)}, u32[]{:S(2)}, u32[]{:S(2)}) async-start(bf16[8,128,256]{2,1,0:T(8,128)(2,1)} %pack.3), calls=%async_computation.1 | async-start | bytes 1048576 | tf_op jit(solution)/shard_map/all_to_all | solution.py:287
  26.6 9.5 %collective-permute-start.1 = (bf16[3,128,256]{2,1,0:T(8,128)(2,1)S(1)}, bf16[3,128,256]{2,1,0:T(8,128)(2,1)S(1)}, u32[]{:S(2)}, u32[]{:S(2)}) collective-permute-start(bf16[3,128,256]{2,1,0:T(8,128)(2,1)S(1)} %get-tuple-element.31), channel_id=1, source_target_pairs={{8,0},{16,8},{24,16},{32,24},{40,32},{48,40},{56,48},{9,1},{17,9},... | collective-permute-start | bytes 589832 | tf_op jit(solution)/shard_map/ppermute | solution.py:292
  27.9 8.2 %collective-permute-start = (bf16[3,128,256]{2,1,0:T(8,128)(2,1)S(1)}, bf16[3,128,256]{2,1,0:T(8,128)(2,1)S(1)}, u32[]{:S(2)}, u32[]{:S(2)}) collective-permute-start(bf16[3,128,256]{2,1,0:T(8,128)(2,1)S(1)} %get-tuple-element.32), channel_id=1, source_target_pairs={{0,8},{8,16},{16,24},{24,32},{32,40},{40,48},{48,56},{1,9},{9,17},... | collective-permute-start | bytes 589832 | tf_op jit(solution)/shard_map/ppermute | solution.py:292
  45.8 0.8 copy-start
  46.7 0.8 copy-start.1
  48.2 26.2 %all-to-all-start.2 = ((f32[16,2,896]{2,1,0:T(2,128)}), f32[16,2,896]{2,1,0:T(2,128)S(1)}, u32[]{:S(2)}, u32[]{:S(2)}) async-start(f32[16,2,896]{2,1,0:T(2,128)} %broadcast_in_dim.7), calls=%async_computation.2 | async-start | bytes 229376 | tf_op jit(solution)/shard_map/all_to_all | solution.py:287
  59.4 9.8 %collective-permute-start.2 = (bf16[384,256]{1,0:T(8,128)(2,1)S(1)}, bf16[384,256]{1,0:T(8,128)(2,1)S(1)}, u32[]{:S(2)}, u32[]{:S(2)}) collective-permute-start(bf16[384,256]{1,0:T(8,128)(2,1)S(1)} %get-tuple-element.20), channel_id=1, source_target_pairs={{0,8},{8,16},{16,24},{24,32},{32,40},{40,48},{48,56},{1,9},{9,17},... | collective-permute-start | bytes 589832 | tf_op jit(solution)/shard_map/ppermute | solution.py:292
  62.6 8.6 %collective-permute-start.3 = (bf16[384,256]{1,0:T(8,128)(2,1)S(1)}, bf16[384,256]{1,0:T(8,128)(2,1)S(1)}, u32[]{:S(2)}, u32[]{:S(2)}) collective-permute-start(bf16[384,256]{1,0:T(8,128)(2,1)S(1)} %get-tuple-element.21), channel_id=1, source_target_pairs={{8,0},{16,8},{24,16},{32,24},{40,32},{48,40},{56,48},{9,1},{17,9},... | collective-permute-start | bytes 589832 | tf_op jit(solution)/shard_map/ppermute | solution.py:292
  69.2 2.1 %copy-start.3 = (bf16[384,256]{1,0:T(8,128)(2,1)}, bf16[384,256]{1,0:T(8,128)(2,1)S(1)}, u32[]{:S(2)}) copy-start(bf16[384,256]{1,0:T(8,128)(2,1)S(1)} %collective-permute-done.2.from_left) | copy-start | bytes 589828
  71.3 0.7 copy-start.4
  74.3 21.2 %all-to-all-start.3 = ((bf16[8,128,512]{2,1,0:T(8,128)(2,1)}), bf16[8,128,512]{2,1,0:T(8,128)(2,1)S(1)}, u32[]{:S(2)}, u32[]{:S(2)}) async-start(bf16[8,128,512]{2,1,0:T(8,128)(2,1)} %join.1), calls=%async_computation.3 | async-start | bytes 2097152 | tf_op jit(solution)/shard_map/all_to_all | solution.py:287
  95.6 4.8 %copy-start.2 = (bf16[8,128,512]{2,1,0:T(8,128)(2,1)}, bf16[8,128,512]{2,1,0:T(8,128)(2,1)S(1)}, u32[]{:S(2)}) copy-start(bf16[8,128,512]{2,1,0:T(8,128)(2,1)S(1)} %all-to-all-done.3.merged) | copy-start | bytes 3145732
  96.3 9.0 %all-to-all-start.4 = ((f32[8,2,896]{2,1,0:T(2,128)}), f32[8,2,896]{2,1,0:T(2,128)S(1)}, u32[]{:S(2)}, u32[]{:S(2)}) async-start(f32[8,2,896]{2,1,0:T(2,128)} %broadcast_in_dim.8), calls=%async_computation.4 | async-start | bytes 114688 | tf_op jit(solution)/shard_map/all_to_all | solution.py:287
where the time goes:
time: 107 us; the launch traced here: 106 us
  starting transfers between devices  45.9 us (43%)
  waiting for transfers between devices  25.4 us (24%)
  Pallas kernels  18.4 us (17%)
  blocking collectives  9.4 us (9%)
  local copies, waits for them, and re-layouts  5.99 us (6%)
    all_to_all x5, starting transfers between devices, to_all(): return lax.all_to_all(x, axes, 0, 0, tiled=True)  36 us
    all_to_all x5, waiting for transfers between devices, to_all(): return lax.all_to_all(x, axes, 0, 0, tiled=True)  18 us
    ppermute x4, starting transfers between devices, shifted(): lax.ppermute(x, 'grp', [(i, i + by) for i in range(n) if 0 <= i + by < n])  9.88 us
    pallas_call x1, Pallas kernels, attention(): pl.pallas_call(attention_kernel, out_shape=(jax.ShapeDtypeStruct((ROWS, 2...  9.73 us
    psum x1, blocking collectives, body(): one = lax.psum(jnp.sum(column, axis=0), 'row')  9.4 us
    ppermute x4, waiting for transfers between devices, shifted(): lax.ppermute(x, 'grp', [(i, i + by) for i in range(n) if 0 <= i + by < n])  7.34 us
    pallas_call x2, Pallas kernels, pack(): pl.pallas_call(pack_kernel, out_shape=jax.ShapeDtypeStruct((MEMB, FR, 2 *...  3.84 us
    pallas_call x1, Pallas kernels, unpack(): pl.pallas_call(unpack_kernel, out_shape=(jax.ShapeDtypeStruct((1, FR, MEM...  2.48 us
  transfers between devices with their start and end apart: 9, of which 6 were waited for; matrix products, arithmetic and copies ran while one was open for 2% of the time, Pallas kernels for 6%

commit v1 on v0

--- a/solution.py
+++ b/solution.py
@@ -38,7 +38,7 @@
 
 def attention_kernel(
     place, kv_left, kv_mid, kv_right, qd, bias_row,
-    od, dkv, dkv_left, dkv_right, bias_grad,
+    grads, dkv_left, dkv_right, bias_grad,
     kv, kv_t, qd_t, table, scores, probs, dscores, key_acc, value_acc, diag_acc,
     od_t, sems,
 ):
@@ -164,12 +164,17 @@
         if now[3]:
             now[3].query_grad()
             if now[3].h == 1:
-                od[pl.ds(now[3].base, TILE), :] = od_t[(now[3].base // TILE) % 2].T
+                o, first_block = now[3].o, now[3].base // FR
+                both = od_t[o].T
+                for n in range(TILE // FR):
+                    grads[first_block + n, 0] = both[n * FR : (n + 1) * FR]
 
     for n, acc in enumerate((key_acc, value_acc)):
         cols = slice(n * LANES, (n + 1) * LANES)
         dkv_left[:, cols] = acc[:, :CONTEXT].astype(BF16).T
-        dkv[:, cols] = acc[:, CONTEXT : CONTEXT + ROWS].astype(BF16).T
+        for m in range(MEMB):
+            at = CONTEXT + m * FR
+            grads[m, 1, :, cols] = acc[:, at : at + FR].astype(BF16).T
         dkv_right[:, cols] = acc[:, CONTEXT + ROWS :].astype(BF16).T
 
     wide = (DIAGS + 1) * LANES
@@ -182,23 +187,24 @@
     for step in (4, 2, 1):
         part = jnp.where((sub & step) != 0, pltpu.roll(part, wide - step, 2), part)
     total = jnp.sum(part, axis=1)
-    bias_grad[...] = total[:, LANES:]
-
-
-def attention(place, kv_left, kv_mid, kv_right, qd, bias_row):
+    total = total[:, LANES:]
+    for n in range(bias_grad.shape[0]):
+        bias_grad[n] = total
+
+
+def attention(times, place, kv_left, kv_mid, kv_right, qd, bias_row):
     vmem = pl.BlockSpec(memory_space=pltpu.VMEM)
     hbm = pl.BlockSpec(memory_space=pl.ANY)
     return pl.pallas_call(
         attention_kernel,
         out_shape=(
-            jax.ShapeDtypeStruct((ROWS, 2 * LANES), BF16),
-            jax.ShapeDtypeStruct((ROWS, 2 * LANES), BF16),
+            jax.ShapeDtypeStruct((MEMB, 2, FR, 2 * LANES), BF16),
             jax.ShapeDtypeStruct((CONTEXT, 2 * LANES), BF16),
             jax.ShapeDtypeStruct((CONTEXT, 2 * LANES), BF16),
-            jax.ShapeDtypeStruct((2, DIAGS * LANES), F32),
+            jax.ShapeDtypeStruct((times, 2, DIAGS * LANES), F32),
         ),
         in_specs=[pl.BlockSpec(memory_space=pltpu.SMEM), hbm, hbm, hbm, vmem, vmem],
-        out_specs=(vmem,) * 5,
+        out_specs=(vmem,) * 4,
         scratch_shapes=[
             pltpu.VMEM((PAD_ROWS, 2 * LANES), BF16),
             pltpu.VMEM((2 * LANES, PAD_ROWS), BF16),
@@ -238,10 +244,16 @@
     )(a, b)
 
 
-def unpack_kernel(merged, *outs):
+def unpack_kernel(merged, *refs):
+    outs, (blocks, sems) = refs[:4], refs[4:]
+    copies = [pltpu.make_async_copy(merged.at[m], blocks.at[m], sems.at[m]) for m in range(MEMB)]
+    for copy in copies:
+        copy.start()
     for m in range(MEMB):
+        copies[m].wait()
         for n, out in enumerate(outs):
-            out[0, :, m * LANES : (m + 1) * LANES] = merged[m, :, n * LANES : (n + 1) * LANES]
+            at = slice((n % 2) * LANES, (n % 2 + 1) * LANES)
+            out[0, :, m * LANES : (m + 1) * LANES] = blocks[m, n // 2, :, at]
 
 
 def unpack(merged):
@@ -249,38 +261,55 @@
     return pl.pallas_call(
         unpack_kernel,
         out_shape=(jax.ShapeDtypeStruct((1, FR, MEMB * LANES), BF16),) * 4,
-        in_specs=[vmem],
+        in_specs=[pl.BlockSpec(memory_space=pl.ANY)],
         out_specs=(vmem,) * 4,
+        scratch_shapes=[
+            pltpu.VMEM((MEMB, 2, FR, 2 * LANES), BF16),
+            pltpu.SemaphoreType.DMA((MEMB,)),
+        ],
         cost_estimate=pl.CostEstimate(flops=0, bytes_accessed=2 * 2**20, transcendentals=0),
         name="unpack",
     )(merged)
 
 
-def join_kernel(od, dkv, from_left, from_right, out):
-    def add(a, b):
-        return (a.astype(F32) + b.astype(F32)).astype(BF16)
-
-    for m in range(MEMB):
-        mine = pl.ds(m * FR, FR)
-        out[m, :, : 2 * LANES] = od[mine]
-        if m < NB:
-            out[m, :, 2 * LANES :] = add(dkv[mine], from_left[mine])
-        elif m >= MEMB - NB:
-            out[m, :, 2 * LANES :] = add(dkv[mine], from_right[pl.ds((m - MEMB + NB) * FR, FR)])
-        else:
-            out[m, :, 2 * LANES :] = dkv[mine]
-
-
-def join(od, dkv, from_left, from_right):
-    vmem = pl.BlockSpec(memory_space=pltpu.VMEM)
+def join_kernel(grads, from_left, from_right, out, own, far, sems):
+    del grads
+    halves = ((pl.ds(0, NB), from_left), (pl.ds(MEMB - NB, NB), from_right))
+    loads = []
+    for n, (at, halo) in enumerate(halves):
+        loads.append(
+            (
+                pltpu.make_async_copy(out.at[at, 1], own.at[n], sems.at[2 * n]),
+                pltpu.make_async_copy(halo, far.at[n], sems.at[2 * n + 1]),
+            )
+        )
+    for pair in loads:
+        for copy in pair:
+            copy.start()
+    stores = []
+    for n, (at, halo) in enumerate(halves):
+        for copy in loads[n]:
+            copy.wait()
+        own[n] = (own[n].astype(F32) + far[n].astype(F32)).astype(BF16)
+        stores.append(pltpu.make_async_copy(own.at[n], out.at[at, 1], sems.at[4 + n]))
+        stores[-1].start()
+    for copy in stores:
+        copy.wait()
+
+
+def join(grads, from_left, from_right):
+    hbm = pl.BlockSpec(memory_space=pl.ANY)
+    half = pltpu.VMEM((2, NB, FR, 2 * LANES), BF16)
     return pl.pallas_call(
         join_kernel,
-        out_shape=jax.ShapeDtypeStruct((MEMB, FR, 4 * LANES), BF16),
-        in_specs=[vmem] * 4,
-        out_specs=vmem,
-        cost_estimate=pl.CostEstimate(flops=2**18, bytes_accessed=2 * 2**20, transcendentals=0),
+        out_shape=jax.ShapeDtypeStruct((MEMB, 2, FR, 2 * LANES), BF16),
+        in_specs=[hbm] * 3,
+        out_specs=hbm,
+        scratch_shapes=[half, half, pltpu.SemaphoreType.DMA((6,))],
+        input_output_aliases={0: 0},
+        cost_estimate=pl.CostEstimate(flops=2**18, bytes_accessed=2**20, transcendentals=0),
         name="join",
-    )(od, dkv, from_left, from_right)
+    )(grads, from_left, from_right)
 
 
 def to_all(x, axes):
@@ -303,7 +332,9 @@
     gap = jnp.full((2, 2 * TILE - 1), EXCLUDED, F32)
     bias_row = jnp.concatenate([mine[:, 2 * CONTEXT :], gap, mine[:, : 2 * CONTEXT]], axis=1)
     place = jnp.stack([lax.axis_index("grp"), jnp.int32(groups)])
-    od, dkv, dleft, dright, dbias = attention(
+    column = lax.axis_size(("far", "grp"))
+    grads, dleft, dright, dbias = attention(
+        column,
         place,
         left.reshape(CONTEXT, 2 * LANES),
         kv.reshape(ROWS, 2 * LANES),
@@ -311,11 +342,11 @@
         qd.reshape(ROWS, 2 * LANES),
         bias_row,
     )
-    from_right = shifted(dleft, -1)
-    from_left = shifted(dright, 1)
-    column = lax.axis_size(("far", "grp"))
-    column = to_all(jnp.broadcast_to(dbias[None], (column,) + dbias.shape), ("far", "grp"))
-    grads = join(od, dkv, from_left, from_right)
+    halo = (NB, FR, 2 * LANES)
+    from_right = shifted(dleft.reshape(halo), -1)
+    from_left = shifted(dright.reshape(halo), 1)
+    column = to_all(dbias, ("far", "grp"))
+    grads = join(grads, from_left, from_right)
     grads, column = lax.optimization_barrier((grads, column))
     merged = to_all(grads, ("x", "core"))
     one = lax.psum(jnp.sum(column, axis=0), "row")

time: 107 us -> 106 us (level)
  local copies, waits for them, and re-layouts: 5.99 us -> 4.65 us
    unnamed x10 -> x8, local copies, waits for them, and re-layouts: 2.32 us -> 1.65 us
where the time goes in v1:
time: 106 us; the launch traced here: 105 us
  starting transfers between devices  45.9 us (43%)
  waiting for transfers between devices  25.5 us (24%)
  Pallas kernels  18.6 us (18%)
  blocking collectives  9.41 us (9%)
  local copies, waits for them, and re-layouts  4.65 us (4%)
    all_to_all x5, starting transfers between devices, to_all(): return lax.all_to_all(x, axes, 0, 0, tiled=True)  36 us
    all_to_all x5, waiting for transfers between devices, to_all(): return lax.all_to_all(x, axes, 0, 0, tiled=True)  18.1 us
    pallas_call x1, Pallas kernels, attention(): pl.pallas_call(attention_kernel, out_shape=(jax.ShapeDtypeStruct((MEMB, 2...  10.4 us
    ppermute x4, starting transfers between devices, shifted(): lax.ppermute(x, 'grp', [(i, i + by) for i in range(n) if 0 <= i + by < n])  9.88 us
    psum x1, blocking collectives, body(): one = lax.psum(jnp.sum(column, axis=0), 'row')  9.41 us
    ppermute x4, waiting for transfers between devices, shifted(): lax.ppermute(x, 'grp', [(i, i + by) for i in range(n) if 0 <= i + by < n])  7.33 us
    pallas_call x2, Pallas kernels, pack(): pl.pallas_call(pack_kernel, out_shape=jax.ShapeDtypeStruct((MEMB, FR, 2 *...  3.83 us
    pallas_call x1, Pallas kernels, unpack(): pl.pallas_call(unpack_kernel, out_shape=(jax.ShapeDtypeStruct((1, FR, MEM...  2.35 us
  transfers between devices with their start and end apart: 9, of which 6 were waited for; matrix products, arithmetic and copies ran while one was open for 2% of the time, Pallas kernels for 6%

profile of v1, /device:TPU:1, one launch (start us, length us, event | category | flops | bytes accessed | tf_op | source)
XLA Modules:
  0.0 104.9 jit_solution(878216401145511362)
XLA Ops:
  0.6 1.9 %pack.2 = bf16[8,128,256]{2,1,0:T(8,128)(2,1)} custom-call(bf16[1,128,1024]{2,1,0:T(8,128)(2,1)} %a.2, bf16[1,128,1024]{2,1,0:T(8,128)(2,1)} %b.2), custom_call_target="tpu_custom_call" | custom-call | bytes 1048576 | tf_op jit(solution)/shard_map/pack/pallas_call | solution.py:237
  2.5 10.3 %all-to-all-start = ((bf16[8,128,256]{2,1,0:T(8,128)(2,1)}), bf16[8,128,256]{2,1,0:T(8,128)(2,1)S(1)}, u32[]{:S(2)}, u32[]{:S(2)}) async-start(bf16[8,128,256]{2,1,0:T(8,128)(2,1)} %pack.2), calls=%async_computation | async-start | bytes 1048576 | tf_op jit(solution)/shard_map/all_to_all | solution.py:316
  12.8 1.9 %pack.3 = bf16[8,128,256]{2,1,0:T(8,128)(2,1)} custom-call(bf16[1,128,1024]{2,1,0:T(8,128)(2,1)} %a.3, bf16[1,128,1024]{2,1,0:T(8,128)(2,1)} %b.3), custom_call_target="tpu_custom_call" | custom-call | bytes 1048576 | tf_op jit(solution)/shard_map/pack/pallas_call | solution.py:237
  14.7 0.8 dynamic-slice
  15.5 6.8 %all-to-all-done = bf16[8,128,256]{2,1,0:T(8,128)(2,1)S(1)} async-done(((bf16[8,128,256]{2,1,0:T(8,128)(2,1)}), bf16[8,128,256]{2,1,0:T(8,128)(2,1)S(1)}, u32[]{:S(2)}, u32[]{:S(2)}) %all-to-all-start) | async-done | bytes 524320 | tf_op jit(solution)/shard_map/all_to_all | solution.py:316
  22.3 4.3 %all-to-all-start.1 = ((bf16[8,128,256]{2,1,0:T(8,128)(2,1)}), bf16[8,128,256]{2,1,0:T(8,128)(2,1)S(1)}, u32[]{:S(2)}, u32[]{:S(2)}) async-start(bf16[8,128,256]{2,1,0:T(8,128)(2,1)} %pack.3), calls=%async_computation.1 | async-start | bytes 1048576 | tf_op jit(solution)/shard_map/all_to_all | solution.py:316
  26.6 1.3 %collective-permute-start.1 = (bf16[3,128,256]{2,1,0:T(8,128)(2,1)S(1)}, bf16[3,128,256]{2,1,0:T(8,128)(2,1)S(1)}, u32[]{:S(2)}, u32[]{:S(2)}) collective-permute-start(bf16[3,128,256]{2,1,0:T(8,128)(2,1)S(1)} %get-tuple-element.29), channel_id=1, source_target_pairs={{8,0},{16,8},{24,16},{32,24},{40,32},{48,40},{56,48},{9,1},{17,9},... | collective-permute-start | bytes 589832 | tf_op jit(solution)/shard_map/ppermute | solution.py:321
  27.9 4.0 %collective-permute-start = (bf16[3,128,256]{2,1,0:T(8,128)(2,1)S(1)}, bf16[3,128,256]{2,1,0:T(8,128)(2,1)S(1)}, u32[]{:S(2)}, u32[]{:S(2)}) collective-permute-start(bf16[3,128,256]{2,1,0:T(8,128)(2,1)S(1)} %get-tuple-element.30), channel_id=1, source_target_pairs={{0,8},{8,16},{16,24},{24,32},{32,40},{40,48},{48,56},{1,9},{9,17},... | collective-permute-start | bytes 589832 | tf_op jit(solution)/shard_map/ppermute | solution.py:321
  31.9 0.8 constant_dynamic-slice_fusion
  32.7 0.1 concatenate.3.bias_row
  32.8 0.1 pad_add_fusion.place
  32.9 3.2 %all-to-all-done.1 = bf16[8,128,256]{2,1,0:T(8,128)(2,1)S(1)} async-done(((bf16[8,128,256]{2,1,0:T(8,128)(2,1)}), bf16[8,128,256]{2,1,0:T(8,128)(2,1)S(1)}, u32[]{:S(2)}, u32[]{:S(2)}) %all-to-all-start.1) | async-done | bytes 524320 | tf_op jit(solution)/shard_map/all_to_all | solution.py:316
  36.1 0.0 collective-permute-done.1
  36.1 0.0 collective-permute-done
  36.1 10.4 %attention.1 = (bf16[8,2,128,256]{3,2,1,0:T(8,128)(2,1)S(1)}, bf16[384,256]{1,0:T(8,128)(2,1)S(1)}, bf16[384,256]{1,0:T(8,128)(2,1)S(1)}, f32[16,2,896]{2,1,0:T(2,128)}) custom-call(s32[2]{0:T(128)S(1)} %pad_add_fusion.place, bf16[384,256]{1,0:T(8,128)(2,1)S(1)} %bitcast.11, bf16[1024,256]{1,0:T(8,128)(2,1)S(1)} %bitcast.8, bf16[384,256]{1,0:T(8,128)(2,1)S(1)} %bitcast.10, ...), custom_call_target="tpu_custom_call" | custom-call | flops 3000000000 | bytes 6291456 | tf_op jit(solution)/shard_map/attention/pallas_call | solution.py:198
  46.5 0.0 copy-start
  46.5 1.0 copy-done
  47.5 11.2 %all-to-all-start.2 = ((f32[16,2,896]{2,1,0:T(2,128)}), f32[16,2,896]{2,1,0:T(2,128)S(1)}, u32[]{:S(2)}, u32[]{:S(2)}) async-start(f32[16,2,896]{2,1,0:T(2,128)} %get-tuple-element.20), calls=%async_computation.2 | async-start | bytes 229376 | tf_op jit(solution)/shard_map/all_to_all | solution.py:316
  58.7 3.3 %collective-permute-start.2 = (bf16[3,128,256]{2,1,0:T(8,128)(2,1)S(1)}, bf16[3,128,256]{2,1,0:T(8,128)(2,1)S(1)}, u32[]{:S(2)}, u32[]{:S(2)}) collective-permute-start(bf16[3,128,256]{2,1,0:T(8,128)(2,1)S(1)} %bitcast.13), channel_id=1, source_target_pairs={{0,8},{8,16},{16,24},{24,32},{32,40},{40,48},{48,56},{1,9},{9,17},... | collective-permute-start | bytes 589832 | tf_op jit(solution)/shard_map/ppermute | solution.py:321
  62.0 1.3 %collective-permute-start.3 = (bf16[3,128,256]{2,1,0:T(8,128)(2,1)S(1)}, bf16[3,128,256]{2,1,0:T(8,128)(2,1)S(1)}, u32[]{:S(2)}, u32[]{:S(2)}) collective-permute-start(bf16[3,128,256]{2,1,0:T(8,128)(2,1)S(1)} %bitcast.12), channel_id=1, source_target_pairs={{8,0},{16,8},{24,16},{32,24},{40,32},{48,40},{56,48},{9,1},{17,9},... | collective-permute-start | bytes 589832 | tf_op jit(solution)/shard_map/ppermute | solution.py:321
  63.3 5.3 %collective-permute-done.2.from_left = bf16[3,128,256]{2,1,0:T(8,128)(2,1)S(1)} collective-permute-done((bf16[3,128,256]{2,1,0:T(8,128)(2,1)S(1)}, bf16[3,128,256]{2,1,0:T(8,128)(2,1)S(1)}, u32[]{:S(2)}, u32[]{:S(2)}) %collective-permute-start.2) | collective-permute-done | bytes 196640 | tf_op jit(solution)/shard_map/ppermute | solution.py:321
  68.5 0.0 copy-start.2
  68.5 2.1 %collective-permute-done.3.from_right = bf16[3,128,256]{2,1,0:T(8,128)(2,1)S(1)} collective-permute-done((bf16[3,128,256]{2,1,0:T(8,128)(2,1)S(1)}, bf16[3,128,256]{2,1,0:T(8,128)(2,1)S(1)}, u32[]{:S(2)}, u32[]{:S(2)}) %collective-permute-start.3) | collective-permute-done | bytes 196640 | tf_op jit(solution)/shard_map/ppermute | solution.py:321
  70.6 0.0 copy-start.3
  70.6 0.0 copy-done.2
  70.6 0.7 copy-done.3
  71.3 2.0 %join.1 = bf16[8,2,128,256]{3,2,1,0:T(8,128)(2,1)} custom-call(bf16[8,2,128,256]{3,2,1,0:T(8,128)(2,1)} %copy-done, bf16[3,128,256]{2,1,0:T(8,128)(2,1)} %copy-done.2, bf16[3,128,256]{2,1,0:T(8,128)(2,1)} %copy-done.3), custom_call_target="tpu_custom_call", output_to_operand_aliasing={{}: (0, {})} | custom-call | flops 262144 | bytes 1048576 | tf_op jit(solution)/shard_map/join/pallas_call | solution.py:303
  73.3 0.0 all-to-all-done.2
  73.3 6.2 %all-to-all-start.3 = ((bf16[8,2,128,256]{3,2,1,0:T(8,128)(2,1)}), bf16[8,2,128,256]{3,2,1,0:T(8,128)(2,1)S(1)}, u32[]{:S(2)}, u32[]{:S(2)}) async-start(bf16[8,2,128,256]{3,2,1,0:T(8,128)(2,1)} %join.1), calls=%async_computation.3 | async-start | bytes 2097152 | tf_op jit(solution)/shard_map/all_to_all | solution.py:316
  79.5 0.1 reduce_sum.9
  79.5 9.4 %psum.7 = f32[2,896]{1,0:T(2,128)S(1)} all-reduce(f32[2,896]{1,0:T(2,128)S(1)} %reduce_sum.9), channel_id=1, replica_groups=mesh['far'=2,'row'=4,'grp'=8,'x'=4,'core'=2] {'row'}, use_global_device_ids=true, to_apply=%region_1.0 | all-reduce | flops 1792 | bytes 14336 | tf_op jit(solution)/shard_map/psum | solution.py:352
  88.9 5.6 %all-to-all-done.3.merged = bf16[8,2,128,256]{3,2,1,0:T(8,128)(2,1)S(1)} async-done(((bf16[8,2,128,256]{3,2,1,0:T(8,128)(2,1)}), bf16[8,2,128,256]{3,2,1,0:T(8,128)(2,1)S(1)}, u32[]{:S(2)}, u32[]{:S(2)}) %all-to-all-start.3) | async-done | bytes 1048608 | tf_op jit(solution)/shard_map/all_to_all | solution.py:316
  94.6 0.0 copy-start.1
  94.6 0.7 broadcast_in_dim.10
  95.3 4.1 %all-to-all-start.4 = ((f32[8,2,896]{2,1,0:T(2,128)}), f32[8,2,896]{2,1,0:T(2,128)S(1)}, u32[]{:S(2)}, u32[]{:S(2)}) async-start(f32[8,2,896]{2,1,0:T(2,128)} %broadcast_in_dim.10), calls=%async_computation.4 | async-start | bytes 114688 | tf_op jit(solution)/shard_map/all_to_all | solution.py:316
  99.4 0.0 copy-done.1
  99.4 2.3 %unpack.1 = (bf16[1,128,1024]{2,1,0:T(8,128)(2,1)}, bf16[1,128,1024]{2,1,0:T(8,128)(2,1)}, bf16[1,128,1024]{2,1,0:T(8,128)(2,1)}, bf16[1,128,1024]{2,1,0:T(8,128)(2,1)}) custom-call(bf16[8,2,128,256]{3,2,1,0:T(8,128)(2,1)} %copy-done.1), custom_call_target="tpu_custom_call" | custom-call | bytes 2097152 | tf_op jit(solution)/shard_map/unpack/pallas_call | solution.py:261
  101.7 2.5 %all-to-all-done.4 = f32[8,2,896]{2,1,0:T(2,128)S(1)} async-done(((f32[8,2,896]{2,1,0:T(2,128)}), f32[8,2,896]{2,1,0:T(2,128)S(1)}, u32[]{:S(2)}, u32[]{:S(2)}) %all-to-all-start.4) | async-done | bytes 57376 | tf_op jit(solution)/shard_map/all_to_all | solution.py:316
  104.2 0.7 reshape.38
  (2 shorter events, 0.0 us)
Async XLA Ops:
  2.5 19.8 %all-to-all-start = ((bf16[8,128,256]{2,1,0:T(8,128)(2,1)}), bf16[8,128,256]{2,1,0:T(8,128)(2,1)S(1)}, u32[]{:S(2)}, u32[]{:S(2)}) async-start(bf16[8,128,256]{2,1,0:T(8,128)(2,1)} %pack.2), calls=%async_computation | async-start | bytes 1048576 | tf_op jit(solution)/shard_map/all_to_all | solution.py:316
  22.3 13.8 %all-to-all-start.1 = ((bf16[8,128,256]{2,1,0:T(8,128)(2,1)}), bf16[8,128,256]{2,1,0:T(8,128)(2,1)S(1)}, u32[]{:S(2)}, u32[]{:S(2)}) async-start(bf16[8,128,256]{2,1,0:T(8,128)(2,1)} %pack.3), calls=%async_computation.1 | async-start | bytes 1048576 | tf_op jit(solution)/shard_map/all_to_all | solution.py:316
  26.6 9.5 %collective-permute-start.1 = (bf16[3,128,256]{2,1,0:T(8,128)(2,1)S(1)}, bf16[3,128,256]{2,1,0:T(8,128)(2,1)S(1)}, u32[]{:S(2)}, u32[]{:S(2)}) collective-permute-start(bf16[3,128,256]{2,1,0:T(8,128)(2,1)S(1)} %get-tuple-element.29), channel_id=1, source_target_pairs={{8,0},{16,8},{24,16},{32,24},{40,32},{48,40},{56,48},{9,1},{17,9},... | collective-permute-start | bytes 589832 | tf_op jit(solution)/shard_map/ppermute | solution.py:321
  27.9 8.2 %collective-permute-start = (bf16[3,128,256]{2,1,0:T(8,128)(2,1)S(1)}, bf16[3,128,256]{2,1,0:T(8,128)(2,1)S(1)}, u32[]{:S(2)}, u32[]{:S(2)}) collective-permute-start(bf16[3,128,256]{2,1,0:T(8,128)(2,1)S(1)} %get-tuple-element.30), channel_id=1, source_target_pairs={{0,8},{8,16},{16,24},{24,32},{32,40},{40,48},{48,56},{1,9},{9,17},... | collective-permute-start | bytes 589832 | tf_op jit(solution)/shard_map/ppermute | solution.py:321
  46.5 1.0 copy-start
  47.5 25.8 %all-to-all-start.2 = ((f32[16,2,896]{2,1,0:T(2,128)}), f32[16,2,896]{2,1,0:T(2,128)S(1)}, u32[]{:S(2)}, u32[]{:S(2)}) async-start(f32[16,2,896]{2,1,0:T(2,128)} %get-tuple-element.20), calls=%async_computation.2 | async-start | bytes 229376 | tf_op jit(solution)/shard_map/all_to_all | solution.py:316
  58.7 9.8 %collective-permute-start.2 = (bf16[3,128,256]{2,1,0:T(8,128)(2,1)S(1)}, bf16[3,128,256]{2,1,0:T(8,128)(2,1)S(1)}, u32[]{:S(2)}, u32[]{:S(2)}) collective-permute-start(bf16[3,128,256]{2,1,0:T(8,128)(2,1)S(1)} %bitcast.13), channel_id=1, source_target_pairs={{0,8},{8,16},{16,24},{24,32},{32,40},{40,48},{48,56},{1,9},{9,17},... | collective-permute-start | bytes 589832 | tf_op jit(solution)/shard_map/ppermute | solution.py:321
  62.0 8.6 %collective-permute-start.3 = (bf16[3,128,256]{2,1,0:T(8,128)(2,1)S(1)}, bf16[3,128,256]{2,1,0:T(8,128)(2,1)S(1)}, u32[]{:S(2)}, u32[]{:S(2)}) collective-permute-start(bf16[3,128,256]{2,1,0:T(8,128)(2,1)S(1)} %bitcast.12), channel_id=1, source_target_pairs={{8,0},{16,8},{24,16},{32,24},{40,32},{48,40},{56,48},{9,1},{17,9},... | collective-permute-start | bytes 589832 | tf_op jit(solution)/shard_map/ppermute | solution.py:321
  68.5 2.1 %copy-start.2 = (bf16[3,128,256]{2,1,0:T(8,128)(2,1)}, bf16[3,128,256]{2,1,0:T(8,128)(2,1)S(1)}, u32[]{:S(2)}) copy-start(bf16[3,128,256]{2,1,0:T(8,128)(2,1)S(1)} %collective-permute-done.2.from_left) | copy-start | bytes 589828
  70.6 0.7 copy-start.3
  73.3 21.3 %all-to-all-start.3 = ((bf16[8,2,128,256]{3,2,1,0:T(8,128)(2,1)}), bf16[8,2,128,256]{3,2,1,0:T(8,128)(2,1)S(1)}, u32[]{:S(2)}, u32[]{:S(2)}) async-start(bf16[8,2,128,256]{3,2,1,0:T(8,128)(2,1)} %join.1), calls=%async_computation.3 | async-start | bytes 2097152 | tf_op jit(solution)/shard_map/all_to_all | solution.py:316
  94.6 4.8 %copy-start.1 = (bf16[8,2,128,256]{3,2,1,0:T(8,128)(2,1)}, bf16[8,2,128,256]{3,2,1,0:T(8,128)(2,1)S(1)}, u32[]{:S(2)}) copy-start(bf16[8,2,128,256]{3,2,1,0:T(8,128)(2,1)S(1)} %all-to-all-done.3.merged) | copy-start | bytes 3145732
  95.3 9.0 %all-to-all-start.4 = ((f32[8,2,896]{2,1,0:T(2,128)}), f32[8,2,896]{2,1,0:T(2,128)S(1)}, u32[]{:S(2)}, u32[]{:S(2)}) async-start(f32[8,2,896]{2,1,0:T(2,128)} %broadcast_in_dim.10), calls=%async_computation.4 | async-start | bytes 114688 | tf_op jit(solution)/shard_map/all_to_all | solution.py:316

commit v2 on v1

--- a/solution.py
+++ b/solution.py
@@ -55,15 +55,19 @@
     value_acc[...] = jnp.zeros_like(value_acc)
     diag_acc[...] = jnp.zeros_like(diag_acc)
     for h in range(2):
-        for c in range(NCH):
-            start = (-LANES * (c + 1)) % (5 * TILE)
+        dead = jnp.full((CH, LANES), EXCLUDED, F32)
+        table[h, pl.ds(0, CH), LANES:] = dead
+        table[h, pl.ds(DIAGS * CH, CH), :LANES] = dead
+        for c in range(DIAGS):
+            start = 5 * TILE - LANES * (c + 1)
             parts = [
-                bias_row[h : h + 1, (start + LANES * n) % (5 * TILE) : (start + LANES * n) % (5 * TILE) + LANES]
-                for n in range(3)
+                bias_row[h : h + 1, at : at + LANES]
+                for at in (start, (start + LANES) % (5 * TILE))
             ]
-            wide = jnp.broadcast_to(jnp.concatenate(parts, axis=1), (CH, 3 * LANES))
-            turned = pltpu.roll(wide, 0, 1, stride=1, stride_axis=0)
-            table[h, pl.ds(c * CH, CH), :] = turned[:, LANES:]
+            wide = jnp.broadcast_to(jnp.concatenate(parts, axis=1), (CH, 2 * LANES))
+            tile = pltpu.roll(wide, 0, 1, stride=1, stride_axis=0)[:, LANES:]
+            table[h, pl.ds(c * CH, CH), :LANES] = tile
+            table[h, pl.ds((c + 1) * CH, CH), LANES:] = tile
     qd_t[...] = qd[...].T
     for copy in copies:
         copy.wait()

time: 106 us -> 105 us (level)
  no operation moved by 1% of the time
where the time goes in v2:
time: 105 us; the launch traced here: 104 us
  starting transfers between devices  45.9 us (44%)
  waiting for transfers between devices  25.5 us (24%)
  Pallas kernels  18.2 us (17%)
  blocking collectives  9.41 us (9%)
  local copies, waits for them, and re-layouts  4.65 us (4%)
    all_to_all x5, starting transfers between devices, to_all(): return lax.all_to_all(x, axes, 0, 0, tiled=True)  36 us
    all_to_all x5, waiting for transfers between devices, to_all(): return lax.all_to_all(x, axes, 0, 0, tiled=True)  18.1 us
    pallas_call x1, Pallas kernels, attention(): pl.pallas_call(attention_kernel, out_shape=(jax.ShapeDtypeStruct((MEMB, 2...  10 us
    ppermute x4, starting transfers between devices, shifted(): lax.ppermute(x, 'grp', [(i, i + by) for i in range(n) if 0 <= i + by < n])  9.88 us
    psum x1, blocking collectives, body(): one = lax.psum(jnp.sum(column, axis=0), 'row')  9.41 us
    ppermute x4, waiting for transfers between devices, shifted(): lax.ppermute(x, 'grp', [(i, i + by) for i in range(n) if 0 <= i + by < n])  7.33 us
    pallas_call x2, Pallas kernels, pack(): pl.pallas_call(pack_kernel, out_shape=jax.ShapeDtypeStruct((MEMB, FR, 2 *...  3.83 us
    pallas_call x1, Pallas kernels, unpack(): pl.pallas_call(unpack_kernel, out_shape=(jax.ShapeDtypeStruct((1, FR, MEM...  2.35 us
  transfers between devices with their start and end apart: 9, of which 6 were waited for; matrix products, arithmetic and copies ran while one was open for 2% of the time, Pallas kernels for 6%

profile of v2, /device:TPU:1, one launch (start us, length us, event | category | flops | bytes accessed | tf_op | source)
XLA Modules:
  0.0 104.5 jit_solution(9833442954861117744)
XLA Ops:
  0.6 1.9 %pack.2 = bf16[8,128,256]{2,1,0:T(8,128)(2,1)} custom-call(bf16[1,128,1024]{2,1,0:T(8,128)(2,1)} %a.2, bf16[1,128,1024]{2,1,0:T(8,128)(2,1)} %b.2), custom_call_target="tpu_custom_call" | custom-call | bytes 1048576 | tf_op jit(solution)/shard_map/pack/pallas_call | solution.py:241
  2.5 10.3 %all-to-all-start = ((bf16[8,128,256]{2,1,0:T(8,128)(2,1)}), bf16[8,128,256]{2,1,0:T(8,128)(2,1)S(1)}, u32[]{:S(2)}, u32[]{:S(2)}) async-start(bf16[8,128,256]{2,1,0:T(8,128)(2,1)} %pack.2), calls=%async_computation | async-start | bytes 1048576 | tf_op jit(solution)/shard_map/all_to_all | solution.py:320
  12.8 1.9 %pack.3 = bf16[8,128,256]{2,1,0:T(8,128)(2,1)} custom-call(bf16[1,128,1024]{2,1,0:T(8,128)(2,1)} %a.3, bf16[1,128,1024]{2,1,0:T(8,128)(2,1)} %b.3), custom_call_target="tpu_custom_call" | custom-call | bytes 1048576 | tf_op jit(solution)/shard_map/pack/pallas_call | solution.py:241
  14.7 0.8 dynamic-slice
  15.5 6.8 %all-to-all-done = bf16[8,128,256]{2,1,0:T(8,128)(2,1)S(1)} async-done(((bf16[8,128,256]{2,1,0:T(8,128)(2,1)}), bf16[8,128,256]{2,1,0:T(8,128)(2,1)S(1)}, u32[]{:S(2)}, u32[]{:S(2)}) %all-to-all-start) | async-done | bytes 524320 | tf_op jit(solution)/shard_map/all_to_all | solution.py:320
  22.3 4.3 %all-to-all-start.1 = ((bf16[8,128,256]{2,1,0:T(8,128)(2,1)}), bf16[8,128,256]{2,1,0:T(8,128)(2,1)S(1)}, u32[]{:S(2)}, u32[]{:S(2)}) async-start(bf16[8,128,256]{2,1,0:T(8,128)(2,1)} %pack.3), calls=%async_computation.1 | async-start | bytes 1048576 | tf_op jit(solution)/shard_map/all_to_all | solution.py:320
  26.6 1.3 %collective-permute-start.1 = (bf16[3,128,256]{2,1,0:T(8,128)(2,1)S(1)}, bf16[3,128,256]{2,1,0:T(8,128)(2,1)S(1)}, u32[]{:S(2)}, u32[]{:S(2)}) collective-permute-start(bf16[3,128,256]{2,1,0:T(8,128)(2,1)S(1)} %get-tuple-element.29), channel_id=1, source_target_pairs={{8,0},{16,8},{24,16},{32,24},{40,32},{48,40},{56,48},{9,1},{17,9},... | collective-permute-start | bytes 589832 | tf_op jit(solution)/shard_map/ppermute | solution.py:325
  27.9 4.0 %collective-permute-start = (bf16[3,128,256]{2,1,0:T(8,128)(2,1)S(1)}, bf16[3,128,256]{2,1,0:T(8,128)(2,1)S(1)}, u32[]{:S(2)}, u32[]{:S(2)}) collective-permute-start(bf16[3,128,256]{2,1,0:T(8,128)(2,1)S(1)} %get-tuple-element.30), channel_id=1, source_target_pairs={{0,8},{8,16},{16,24},{24,32},{32,40},{40,48},{48,56},{1,9},{9,17},... | collective-permute-start | bytes 589832 | tf_op jit(solution)/shard_map/ppermute | solution.py:325
  31.9 0.8 constant_dynamic-slice_fusion
  32.7 0.1 concatenate.3.bias_row
  32.8 0.1 pad_add_fusion.place
  32.9 3.2 %all-to-all-done.1 = bf16[8,128,256]{2,1,0:T(8,128)(2,1)S(1)} async-done(((bf16[8,128,256]{2,1,0:T(8,128)(2,1)}), bf16[8,128,256]{2,1,0:T(8,128)(2,1)S(1)}, u32[]{:S(2)}, u32[]{:S(2)}) %all-to-all-start.1) | async-done | bytes 524320 | tf_op jit(solution)/shard_map/all_to_all | solution.py:320
  36.1 0.0 collective-permute-done.1
  36.1 0.0 collective-permute-done
  36.1 10.0 %attention.1 = (bf16[8,2,128,256]{3,2,1,0:T(8,128)(2,1)S(1)}, bf16[384,256]{1,0:T(8,128)(2,1)S(1)}, bf16[384,256]{1,0:T(8,128)(2,1)S(1)}, f32[16,2,896]{2,1,0:T(2,128)}) custom-call(s32[2]{0:T(128)S(1)} %pad_add_fusion.place, bf16[384,256]{1,0:T(8,128)(2,1)S(1)} %bitcast.11, bf16[1024,256]{1,0:T(8,128)(2,1)S(1)} %bitcast.8, bf16[384,256]{1,0:T(8,128)(2,1)S(1)} %bitcast.10, ...), custom_call_target="tpu_custom_call" | custom-call | flops 3000000000 | bytes 6291456 | tf_op jit(solution)/shard_map/attention/pallas_call | solution.py:202
  46.1 0.0 copy-start
  46.1 1.0 copy-done
  47.1 11.2 %all-to-all-start.2 = ((f32[16,2,896]{2,1,0:T(2,128)}), f32[16,2,896]{2,1,0:T(2,128)S(1)}, u32[]{:S(2)}, u32[]{:S(2)}) async-start(f32[16,2,896]{2,1,0:T(2,128)} %get-tuple-element.20), calls=%async_computation.2 | async-start | bytes 229376 | tf_op jit(solution)/shard_map/all_to_all | solution.py:320
  58.3 3.3 %collective-permute-start.2 = (bf16[3,128,256]{2,1,0:T(8,128)(2,1)S(1)}, bf16[3,128,256]{2,1,0:T(8,128)(2,1)S(1)}, u32[]{:S(2)}, u32[]{:S(2)}) collective-permute-start(bf16[3,128,256]{2,1,0:T(8,128)(2,1)S(1)} %bitcast.13), channel_id=1, source_target_pairs={{0,8},{8,16},{16,24},{24,32},{32,40},{40,48},{48,56},{1,9},{9,17},... | collective-permute-start | bytes 589832 | tf_op jit(solution)/shard_map/ppermute | solution.py:325
  61.6 1.3 %collective-permute-start.3 = (bf16[3,128,256]{2,1,0:T(8,128)(2,1)S(1)}, bf16[3,128,256]{2,1,0:T(8,128)(2,1)S(1)}, u32[]{:S(2)}, u32[]{:S(2)}) collective-permute-start(bf16[3,128,256]{2,1,0:T(8,128)(2,1)S(1)} %bitcast.12), channel_id=1, source_target_pairs={{8,0},{16,8},{24,16},{32,24},{40,32},{48,40},{56,48},{9,1},{17,9},... | collective-permute-start | bytes 589832 | tf_op jit(solution)/shard_map/ppermute | solution.py:325
  62.9 5.3 %collective-permute-done.2.from_left = bf16[3,128,256]{2,1,0:T(8,128)(2,1)S(1)} collective-permute-done((bf16[3,128,256]{2,1,0:T(8,128)(2,1)S(1)}, bf16[3,128,256]{2,1,0:T(8,128)(2,1)S(1)}, u32[]{:S(2)}, u32[]{:S(2)}) %collective-permute-start.2) | collective-permute-done | bytes 196640 | tf_op jit(solution)/shard_map/ppermute | solution.py:325
  68.1 0.0 copy-start.2
  68.1 2.1 %collective-permute-done.3.from_right = bf16[3,128,256]{2,1,0:T(8,128)(2,1)S(1)} collective-permute-done((bf16[3,128,256]{2,1,0:T(8,128)(2,1)S(1)}, bf16[3,128,256]{2,1,0:T(8,128)(2,1)S(1)}, u32[]{:S(2)}, u32[]{:S(2)}) %collective-permute-start.3) | collective-permute-done | bytes 196640 | tf_op jit(solution)/shard_map/ppermute | solution.py:325
  70.2 0.0 copy-start.3
  70.2 0.0 copy-done.2
  70.2 0.7 copy-done.3
  70.9 2.0 %join.1 = bf16[8,2,128,256]{3,2,1,0:T(8,128)(2,1)} custom-call(bf16[8,2,128,256]{3,2,1,0:T(8,128)(2,1)} %copy-done, bf16[3,128,256]{2,1,0:T(8,128)(2,1)} %copy-done.2, bf16[3,128,256]{2,1,0:T(8,128)(2,1)} %copy-done.3), custom_call_target="tpu_custom_call", output_to_operand_aliasing={{}: (0, {})} | custom-call | flops 262144 | bytes 1048576 | tf_op jit(solution)/shard_map/join/pallas_call | solution.py:307
  72.9 0.0 all-to-all-done.2
  72.9 6.2 %all-to-all-start.3 = ((bf16[8,2,128,256]{3,2,1,0:T(8,128)(2,1)}), bf16[8,2,128,256]{3,2,1,0:T(8,128)(2,1)S(1)}, u32[]{:S(2)}, u32[]{:S(2)}) async-start(bf16[8,2,128,256]{3,2,1,0:T(8,128)(2,1)} %join.1), calls=%async_computation.3 | async-start | bytes 2097152 | tf_op jit(solution)/shard_map/all_to_all | solution.py:320
  79.1 0.1 reduce_sum.9
  79.1 9.4 %psum.7 = f32[2,896]{1,0:T(2,128)S(1)} all-reduce(f32[2,896]{1,0:T(2,128)S(1)} %reduce_sum.9), channel_id=1, replica_groups=mesh['far'=2,'row'=4,'grp'=8,'x'=4,'core'=2] {'row'}, use_global_device_ids=true, to_apply=%region_1.0 | all-reduce | flops 1792 | bytes 14336 | tf_op jit(solution)/shard_map/psum | solution.py:356
  88.5 5.6 %all-to-all-done.3.merged = bf16[8,2,128,256]{3,2,1,0:T(8,128)(2,1)S(1)} async-done(((bf16[8,2,128,256]{3,2,1,0:T(8,128)(2,1)}), bf16[8,2,128,256]{3,2,1,0:T(8,128)(2,1)S(1)}, u32[]{:S(2)}, u32[]{:S(2)}) %all-to-all-start.3) | async-done | bytes 1048608 | tf_op jit(solution)/shard_map/all_to_all | solution.py:320
  94.2 0.0 copy-start.1
  94.2 0.7 broadcast_in_dim.10
  94.9 4.1 %all-to-all-start.4 = ((f32[8,2,896]{2,1,0:T(2,128)}), f32[8,2,896]{2,1,0:T(2,128)S(1)}, u32[]{:S(2)}, u32[]{:S(2)}) async-start(f32[8,2,896]{2,1,0:T(2,128)} %broadcast_in_dim.10), calls=%async_computation.4 | async-start | bytes 114688 | tf_op jit(solution)/shard_map/all_to_all | solution.py:320
  99.0 0.0 copy-done.1
  99.0 2.3 %unpack.1 = (bf16[1,128,1024]{2,1,0:T(8,128)(2,1)}, bf16[1,128,1024]{2,1,0:T(8,128)(2,1)}, bf16[1,128,1024]{2,1,0:T(8,128)(2,1)}, bf16[1,128,1024]{2,1,0:T(8,128)(2,1)}) custom-call(bf16[8,2,128,256]{3,2,1,0:T(8,128)(2,1)} %copy-done.1), custom_call_target="tpu_custom_call" | custom-call | bytes 2097152 | tf_op jit(solution)/shard_map/unpack/pallas_call | solution.py:265
  101.3 2.5 %all-to-all-done.4 = f32[8,2,896]{2,1,0:T(2,128)S(1)} async-done(((f32[8,2,896]{2,1,0:T(2,128)}), f32[8,2,896]{2,1,0:T(2,128)S(1)}, u32[]{:S(2)}, u32[]{:S(2)}) %all-to-all-start.4) | async-done | bytes 57376 | tf_op jit(solution)/shard_map/all_to_all | solution.py:320
  103.8 0.7 reshape.38
  (2 shorter events, 0.0 us)
Async XLA Ops:
  2.5 19.8 %all-to-all-start = ((bf16[8,128,256]{2,1,0:T(8,128)(2,1)}), bf16[8,128,256]{2,1,0:T(8,128)(2,1)S(1)}, u32[]{:S(2)}, u32[]{:S(2)}) async-start(bf16[8,128,256]{2,1,0:T(8,128)(2,1)} %pack.2), calls=%async_computation | async-start | bytes 1048576 | tf_op jit(solution)/shard_map/all_to_all | solution.py:320
  22.3 13.8 %all-to-all-start.1 = ((bf16[8,128,256]{2,1,0:T(8,128)(2,1)}), bf16[8,128,256]{2,1,0:T(8,128)(2,1)S(1)}, u32[]{:S(2)}, u32[]{:S(2)}) async-start(bf16[8,128,256]{2,1,0:T(8,128)(2,1)} %pack.3), calls=%async_computation.1 | async-start | bytes 1048576 | tf_op jit(solution)/shard_map/all_to_all | solution.py:320
  26.6 9.5 %collective-permute-start.1 = (bf16[3,128,256]{2,1,0:T(8,128)(2,1)S(1)}, bf16[3,128,256]{2,1,0:T(8,128)(2,1)S(1)}, u32[]{:S(2)}, u32[]{:S(2)}) collective-permute-start(bf16[3,128,256]{2,1,0:T(8,128)(2,1)S(1)} %get-tuple-element.29), channel_id=1, source_target_pairs={{8,0},{16,8},{24,16},{32,24},{40,32},{48,40},{56,48},{9,1},{17,9},... | collective-permute-start | bytes 589832 | tf_op jit(solution)/shard_map/ppermute | solution.py:325
  27.9 8.2 %collective-permute-start = (bf16[3,128,256]{2,1,0:T(8,128)(2,1)S(1)}, bf16[3,128,256]{2,1,0:T(8,128)(2,1)S(1)}, u32[]{:S(2)}, u32[]{:S(2)}) collective-permute-start(bf16[3,128,256]{2,1,0:T(8,128)(2,1)S(1)} %get-tuple-element.30), channel_id=1, source_target_pairs={{0,8},{8,16},{16,24},{24,32},{32,40},{40,48},{48,56},{1,9},{9,17},... | collective-permute-start | bytes 589832 | tf_op jit(solution)/shard_map/ppermute | solution.py:325
  46.1 1.0 copy-start
  47.1 25.8 %all-to-all-start.2 = ((f32[16,2,896]{2,1,0:T(2,128)}), f32[16,2,896]{2,1,0:T(2,128)S(1)}, u32[]{:S(2)}, u32[]{:S(2)}) async-start(f32[16,2,896]{2,1,0:T(2,128)} %get-tuple-element.20), calls=%async_computation.2 | async-start | bytes 229376 | tf_op jit(solution)/shard_map/all_to_all | solution.py:320
  58.3 9.8 %collective-permute-start.2 = (bf16[3,128,256]{2,1,0:T(8,128)(2,1)S(1)}, bf16[3,128,256]{2,1,0:T(8,128)(2,1)S(1)}, u32[]{:S(2)}, u32[]{:S(2)}) collective-permute-start(bf16[3,128,256]{2,1,0:T(8,128)(2,1)S(1)} %bitcast.13), channel_id=1, source_target_pairs={{0,8},{8,16},{16,24},{24,32},{32,40},{40,48},{48,56},{1,9},{9,17},... | collective-permute-start | bytes 589832 | tf_op jit(solution)/shard_map/ppermute | solution.py:325
  61.6 8.6 %collective-permute-start.3 = (bf16[3,128,256]{2,1,0:T(8,128)(2,1)S(1)}, bf16[3,128,256]{2,1,0:T(8,128)(2,1)S(1)}, u32[]{:S(2)}, u32[]{:S(2)}) collective-permute-start(bf16[3,128,256]{2,1,0:T(8,128)(2,1)S(1)} %bitcast.12), channel_id=1, source_target_pairs={{8,0},{16,8},{24,16},{32,24},{40,32},{48,40},{56,48},{9,1},{17,9},... | collective-permute-start | bytes 589832 | tf_op jit(solution)/shard_map/ppermute | solution.py:325
  68.1 2.1 %copy-start.2 = (bf16[3,128,256]{2,1,0:T(8,128)(2,1)}, bf16[3,128,256]{2,1,0:T(8,128)(2,1)S(1)}, u32[]{:S(2)}) copy-start(bf16[3,128,256]{2,1,0:T(8,128)(2,1)S(1)} %collective-permute-done.2.from_left) | copy-start | bytes 589828
  70.2 0.7 copy-start.3
  72.9 21.3 %all-to-all-start.3 = ((bf16[8,2,128,256]{3,2,1,0:T(8,128)(2,1)}), bf16[8,2,128,256]{3,2,1,0:T(8,128)(2,1)S(1)}, u32[]{:S(2)}, u32[]{:S(2)}) async-start(bf16[8,2,128,256]{3,2,1,0:T(8,128)(2,1)} %join.1), calls=%async_computation.3 | async-start | bytes 2097152 | tf_op jit(solution)/shard_map/all_to_all | solution.py:320
  94.2 4.8 %copy-start.1 = (bf16[8,2,128,256]{3,2,1,0:T(8,128)(2,1)}, bf16[8,2,128,256]{3,2,1,0:T(8,128)(2,1)S(1)}, u32[]{:S(2)}) copy-start(bf16[8,2,128,256]{3,2,1,0:T(8,128)(2,1)S(1)} %all-to-all-done.3.merged) | copy-start | bytes 3145732
  94.9 9.0 %all-to-all-start.4 = ((f32[8,2,896]{2,1,0:T(2,128)}), f32[8,2,896]{2,1,0:T(2,128)S(1)}, u32[]{:S(2)}, u32[]{:S(2)}) async-start(f32[8,2,896]{2,1,0:T(2,128)} %broadcast_in_dim.10), calls=%async_computation.4 | async-start | bytes 114688 | tf_op jit(solution)/shard_map/all_to_all | solution.py:320
